TPU v7x, 32 devices: a whole 2x2x4 slice. The times are simulated.
32 devices in a mesh: tok: 8 (over z, x), head: 4 (over y, core).
Axes of the slice: x: 2, y: 2, z: 4, core: 2. Of those that a mesh axis runs over, the one named last changes fastest.
Arguments:
- queries: bfloat16 [2048, 3072], P('tok', 'head'), may hold values from -96 to 96
- key_rows: bfloat16 [2048, 512], P('tok', 'head'), may hold values from -6 to 6
- value_rows: bfloat16 [2048, 512], P('tok', 'head'), may hold values from -12 to 12
- tile_mask: int32 [16, 16], P('tok'), may hold values from 0 to 1, as said below
- out_weight: bfloat16 [3072, 6144], P('head'), may hold values from -0.109375 to 0.109375
Outputs:
- mixed: bfloat16 [2048, 6144], P('tok', 'head')
Inputs may be any that keep to these rules, and one draw needn't show every extreme that they name: `tile_mask`: row r keeps key tile r; every row keeps between 1 and 8 tiles, and some row keeps exactly 8.
All inputs are finite; a program needn't handle non-finite values.
Results may differ from a plain program's by a relative error of at most 0.012.
Values may be sent and summed in bfloat16 or wider, within the bound.
A program may use at most 128 MiB of HBM per device.

v0:
```python
import math

import jax
import jax.numpy as jnp
from jax import lax
from jax.sharding import PartitionSpec as P

HD = 128
TILE = 128


NEGATIVE = -1e30
tiles_per_turn = 16


def tile_block(query_tile, key_chosen, value_chosen, shown_tiles, state, score_scale):
    scores = (
        jnp.einsum("qgjd,ckgd->gjqck", query_tile, key_chosen, preferred_element_type=jnp.float32)
        * score_scale
    )
    shown = shown_tiles[None, None, None, :]
    tile_max = jnp.where(shown, jnp.max(scores, axis=-1), NEGATIVE)
    prob_bf = jnp.where(shown[..., None], jnp.exp(scores - tile_max[..., None]), 0.0).astype(
        jnp.bfloat16
    )
    tile_sums = jnp.sum(prob_bf.astype(jnp.float32), axis=-1)
    tile_parts = jnp.einsum(
        "gjqck,ckgd->gjqcd", prob_bf, value_chosen, preferred_element_type=jnp.float32
    )
    running_max, denominator, numerator = state
    new_max = jnp.maximum(running_max, jnp.max(tile_max, axis=-1))
    rescale = jnp.exp(running_max - new_max)
    tile_weight = jnp.where(shown, jnp.exp(tile_max - new_max[..., None]), 0.0)
    denominator = denominator * rescale + jnp.sum(tile_weight * tile_sums, axis=-1)
    numerator = numerator * rescale[..., None] + jnp.sum(
        tile_weight[..., None] * tile_parts, axis=3
    )
    return (new_max, denominator, numerator)


def sweep_piece(state, query_tile, living, key_tiles, value_tiles, score_scale):
    tile_count = living.shape[0]
    block_tiles = min(tiles_per_turn, tile_count)
    ordering = jnp.argsort(1 - living, stable=True)
    live_total = jnp.sum(living)
    turn_count = (live_total + block_tiles - 1) // block_tiles

    def one_turn(turn_index, inner):
        offset = turn_index * block_tiles
        picked = lax.dynamic_slice_in_dim(ordering, offset, block_tiles)
        shown_tiles = offset + jnp.arange(block_tiles, dtype=jnp.int32) < live_total
        return tile_block(
            query_tile,
            jnp.take(key_tiles, picked, axis=0),
            jnp.take(value_tiles, picked, axis=0),
            shown_tiles,
            inner,
            score_scale,
        )

    return lax.fori_loop(0, turn_count, one_turn, state)


def per_device(queries, key_rows, value_rows, tile_mask, out_weight):
    own_rows = queries.shape[0]
    local_heads = queries.shape[1]
    slot_total = own_rows // TILE
    kv_local = key_rows.shape[1] // HD
    group_size = local_heads // HD // kv_local
    score_scale = 1.0 / math.sqrt(HD)
    query_tiles = queries.reshape(slot_total, TILE, kv_local, group_size, HD)
    slot_rows = [tile_mask[number] for number in range(slot_total)]
    slot_queries = [query_tiles[number] for number in range(slot_total)]
    slot_active = [jnp.int32(1) for number in range(slot_total)]
    empty_max = jnp.full((kv_local, group_size, TILE), NEGATIVE, jnp.float32)
    empty_sum = jnp.zeros((kv_local, group_size, TILE), jnp.float32)
    empty_out = jnp.zeros((kv_local, group_size, TILE, HD), jnp.float32)
    initial = tuple(((empty_max, empty_sum, empty_out) for number in range(len(slot_rows))))
    every_key, every_value = (
        lax.all_gather(key_rows, "tok", axis=0, tiled=True),
        lax.all_gather(value_rows, "tok", axis=0, tiled=True),
    )
    tile_count = every_key.shape[0] // TILE
    key_tiles = every_key.reshape(tile_count, TILE, kv_local, HD)
    value_tiles = every_value.reshape(tile_count, TILE, kv_local, HD)
    result = []
    for absorb_number in range(len(slot_rows)):
        living = slot_rows[absorb_number] * slot_active[absorb_number]
        result.append(
            sweep_piece(
                initial[absorb_number],
                slot_queries[absorb_number],
                living,
                key_tiles,
                value_tiles,
                score_scale,
            )
        )
    carries = tuple(result)
    finished = []
    for number in range(len(slot_rows)):
        running_max, denominator, numerator = carries[number]
        safe_sum = jnp.where(denominator > 0, denominator, 1.0)
        attended = numerator / safe_sum[..., None]
        finished.append(
            attended.transpose(2, 0, 1, 3).reshape(TILE, local_heads).astype(jnp.bfloat16)
        )
    own_stack = jnp.stack(finished[:slot_total])
    attention = own_stack.reshape(own_rows, local_heads)
    mixed = lax.psum_scatter(
        lax.dot_general(
            out_weight, attention, (((0,), (1,)), ((), ())), preferred_element_type=jnp.float32
        ).astype(jnp.bfloat16),
        "head",
        scatter_dimension=0,
        tiled=True,
    )
    return mixed.T


def solution(mesh):
    return jax.shard_map(
        per_device,
        mesh=mesh,
        in_specs=(
            P("tok", "head"),
            P("tok", "head"),
            P("tok", "head"),
            P("tok", None),
            P("head", None),
        ),
        out_specs=P("tok", "head"),
        check_vma=False,
    )
```

profile of v0, /device:TPU:0, one launch (start us, length us, event | category | flops | bytes accessed | tf_op | source)
XLA Modules:
  0.0 161.2 jit_solution(17541276726180953449)
XLA Ops:
  6.5 0.0 reduce-scatter.2.cloned.1.call-start
  6.5 1.4 subtract_bitcast_fusion.1
  8.6 1.3 sort.32
  10.5 1.3 sort.31
  11.9 33.3 %all_gather.7 = bf16[2048,128]{1,0:T(8,128)(2,1)S(1)} all-gather(bf16[256,128]{1,0:T(8,128)(2,1)} %param.13), channel_id=1, replica_groups=mesh['tok'=8,'head'=4] {'tok'}, dimensions={0}, use_global_device_ids=true | all-gather | bytes 589824 | tf_op jit(solution)/shard_map/all_gather | solution.py:81
  45.1 31.4 %all_gather.6 = bf16[2048,128]{1,0:T(8,128)(2,1)S(1)} all-gather(bf16[256,128]{1,0:T(8,128)(2,1)} %param.12), channel_id=1, replica_groups=mesh['tok'=8,'head'=4] {'tok'}, dimensions={0}, use_global_device_ids=true | all-gather | bytes 589824 | tf_op jit(solution)/shard_map/all_gather | solution.py:80
  76.5 0.6 gather_fusion.3
  77.2 0.6 gather_fusion.2
  77.9 0.6 gather_fusion.1
  78.5 0.6 gather_fusion
  79.2 1.1 fusion.37
  80.2 0.2 copy.32
  80.4 0.2 copy.22
  80.6 0.2 bitcast_select_fusion
  80.8 12.8 %while.33 = (s32[]{:T(128)}, f32[1,6,128]{2,1,0:T(8,128)S(1)}, f32[1,6,128]{2,1,0:T(8,128)S(1)}, f32[1,6,128,128]{3,2,1,0:T(8,128)S(1)}, s32[]{:T(128)}, /*index...) while((s32[]{:T(128)}, f32[1,6,128]{2,1,0:T(8,128)S(1)}, ...), condition=%wide.region_17.19_spmd, body=%wide.region_11.18_spmd.sunk | while | flops 827476224 | bytes 47396084 | solution.py:61
  80.8 3.6 %bitcast_reduce_fusion.5 = (f32[6,128,16]{1,0,2:T(8,128)S(1)}, f32[16,128,128,6]{2,1,3,0:T(8,128)}) fusion(bf16[128,1,6,128]{3,0,2,1:T(8,128)(2,1)S(1)} %get-tuple-element.525, bf16[16,128,1,128]{3,1,0,2:T(8,128)(2,1)S(1)} %get-tuple-element.524), kind=kOutput, calls=%fused_computation.32.clone.1 | convolution fusion | flops 405786624 | bytes 7061504 | tf_op jit(solution)/shard_map/while/body/qgjd,ckgd->gjqck/dot_general | solution.py:18
  84.5 0.0 copy-start
  84.5 0.8 add_compare_fusion.5
  85.3 0.1 fusion.57
  85.4 4.7 %convert_reduce_fusion.5 = f32[6,128,16]{1,0,2:T(8,128)S(1)} fusion(f32[6,128,16]{1,0,2:T(8,128)S(1)} %get-tuple-element.491, f32[16,128,128,6]{2,1,3,0:T(8,128)} %get-tuple-element.492, pred[16]{0:T(512)(128)(4,1)S(1)} %add_compare_fusion.5), kind=kLoop, calls=%fused_computation.36.clone.1 | loop fusion | flops 9424896 | bytes 6389776 | tf_op jit(solution)/shard_map/while/body/reduce_sum | solution.py:26
  90.1 0.1 multiply_reduce_fusion.5
  90.2 0.0 copy-done
  90.2 3.2 %fusion.59 = f32[6,128,128]{2,1,0:T(8,128)S(1)} fusion(f32[6,128,16]{1,0,2:T(8,128)S(1)} %get-tuple-element.494, bf16[16,128,1,128]{3,1,0,2:T(8,128)(2,1)S(1)} %get-tuple-element.526, f32[16,128,128,6]{2,1,3,0:T(8,128)S(1)} %copy-done, f32[6,128,16]{1,0,2:T(8,128)S(1)} %get-tuple-element.491, pred[16]{0:T(512)(128)(4,1)S(1)} %add_compare_fusion.5), kind=kOutput, calls=%fused_computation.30.clone.1 | convolution fusion | flops 411992064 | bytes 7307280 | tf_op jit(solution)/shard_map/while/body/gjqck,ckgd->gjqcd/dot_general | solution.py:27
  93.4 0.2 bitcast_add_fusion.11
  93.6 0.2 copy.23
  93.8 0.2 copy.31
  94.0 0.2 copy.19
  94.2 0.2 bitcast_select_fusion.2
  94.4 12.6 %while.32 = (s32[]{:T(128)}, f32[1,6,128]{2,1,0:T(8,128)S(1)}, f32[1,6,128]{2,1,0:T(8,128)S(1)}, f32[1,6,128,128]{3,2,1,0:T(8,128)S(1)}, s32[]{:T(128)}, /*index...) while((s32[]{:T(128)}, f32[1,6,128]{2,1,0:T(8,128)S(1)}, ...), condition=%wide.region_8.10_spmd, body=%wide.region_2.9_spmd.sunk | while | flops 827476224 | bytes 47396084 | solution.py:61
  94.4 3.6 %bitcast_reduce_fusion.4 = (f32[6,128,16]{1,0,2:T(8,128)S(1)}, f32[16,128,128,6]{2,1,3,0:T(8,128)}) fusion(bf16[128,1,6,128]{3,0,2,1:T(8,128)(2,1)S(1)} %get-tuple-element.558, bf16[16,128,1,128]{3,1,0,2:T(8,128)(2,1)S(1)} %get-tuple-element.557), kind=kOutput, calls=%fused_computation.7.clone.1 | convolution fusion | flops 405786624 | bytes 7061504 | tf_op jit(solution)/shard_map/while/body/qgjd,ckgd->gjqck/dot_general | solution.py:18
  98.1 0.0 copy-start.1
  98.1 0.7 add_compare_fusion.4
  98.8 0.1 fusion.52
  98.9 4.5 %convert_reduce_fusion.4 = f32[6,128,16]{1,0,2:T(8,128)S(1)} fusion(f32[6,128,16]{1,0,2:T(8,128)S(1)} %get-tuple-element.474, f32[16,128,128,6]{2,1,3,0:T(8,128)} %get-tuple-element.475, pred[16]{0:T(512)(128)(4,1)S(1)} %add_compare_fusion.4), kind=kLoop, calls=%fused_computation.11.clone.1 | loop fusion | flops 9424896 | bytes 6389776 | tf_op jit(solution)/shard_map/while/body/reduce_sum | solution.py:26
  103.4 0.1 multiply_reduce_fusion.4
  103.5 0.0 copy-done.1
  103.5 3.2 %fusion.54 = f32[6,128,128]{2,1,0:T(8,128)S(1)} fusion(f32[6,128,16]{1,0,2:T(8,128)S(1)} %get-tuple-element.477, bf16[16,128,1,128]{3,1,0,2:T(8,128)(2,1)S(1)} %get-tuple-element.559, f32[16,128,128,6]{2,1,3,0:T(8,128)S(1)} %copy-done.1, f32[6,128,16]{1,0,2:T(8,128)S(1)} %get-tuple-element.474, pred[16]{0:T(512)(128)(4,1)S(1)} %add_compare_fusion.4), kind=kOutput, calls=%fused_computation.5.clone.1 | convolution fusion | flops 411992064 | bytes 7307280 | tf_op jit(solution)/shard_map/while/body/gjqck,ckgd->gjqcd/dot_general | solution.py:27
  106.8 0.2 bitcast_add_fusion.9
  107.0 0.2 copy.20
  107.3 0.2 copy.24
  107.5 7.7 %fusion.32 = bf16[6144,256]{0,1:T(8,128)(2,1)} fusion(bf16[256,768]{1,0:T(8,128)(2,1)S(1)} %bitcast.214, bf16[768,6144]{1,0:T(8,128)(2,1)} %param.15), kind=kOutput, calls=%fused_computation.55 | convolution fusion | flops 2417491968 | bytes 12976128 | tf_op jit(solution)/shard_map/dot_general | solution.py:111
  115.2 0.0 reduce-scatter.2.cloned.1.call-update
  115.2 39.2 %reduce-scatter.2.cloned.1.call-done = bf16[1536,256]{0,1:T(8,128)(2,1)} async-done(((bf16[6144,256]{0,1:T(8,128)(2,1)}), bf16[1536,256]{0,1:T(8,128)(2,1)}) %reduce-scatter.2.cloned.1.call-update) | async-done | bytes 786448 | tf_op jit(solution)/shard_map/reduce_scatter | solution.py:110
  (25 shorter events, 0.3 us)
Async XLA Ops:
  6.5 147.9 %reduce-scatter.2.cloned.1.call-start = ((), (), s32[]{:S(2)}) async-start(), calls=%async_computation.1 | async-start | bytes 3932160 | tf_op jit(solution)/shard_map/reduce_scatter | solution.py:110
  84.5 5.7 %copy-start = (f32[16,128,128,6]{2,1,3,0:T(8,128)S(1)}, f32[16,128,128,6]{2,1,3,0:T(8,128)}, u32[]{:S(2)}) copy-start(f32[16,128,128,6]{2,1,3,0:T(8,128)} %get-tuple-element.492) | copy-start | bytes 18874372 | tf_op jit(solution)/shard_map/while
  98.1 5.4 %copy-start.1 = (f32[16,128,128,6]{2,1,3,0:T(8,128)S(1)}, f32[16,128,128,6]{2,1,3,0:T(8,128)}, u32[]{:S(2)}) copy-start(f32[16,128,128,6]{2,1,3,0:T(8,128)} %get-tuple-element.475) | copy-start | bytes 18874372 | tf_op jit(solution)/shard_map/while
Sparse Core Ops, SparseCore 0:
  115.3 39.0 reduce-scatter.1
where the time goes:
time: 161 us
  blocking collectives  64.7 us (40%)
  waiting for transfers between devices  39.2 us (24%)
  matrix products  21.4 us (13%)
  other arithmetic  16 us (10%)
  between operations  14.9 us (9%)
  local copies, waits for them, and re-layouts  4.9 us (3%)
    reduce_scatter x1, waiting for transfers between devices, per_device(): lax.psum_scatter(lax.dot_general(out_weight, attention, (((0,), (1,)), ((...  39.2 us
    all_gather x1, blocking collectives, per_device(): lax.all_gather(value_rows, 'tok', axis=0, tiled=True)  33.3 us
    all_gather x1, blocking collectives, per_device(): lax.all_gather(key_rows, 'tok', axis=0, tiled=True)  31.4 us
    reduce_sum x2, other arithmetic, tile_block(): tile_sums = jnp.sum(prob_bf.astype(jnp.float32), axis=-1)  9.13 us
    dot_general x1, matrix products, per_device(): lax.dot_general(out_weight, attention, (((0,), (1,)), ((), ())), preferre...  7.67 us
    dot_general x2, matrix products, tile_block(): jnp.einsum('qgjd,ckgd->gjqck', query_tile, key_chosen, preferred_element_...  7.29 us
    dot_general x2, matrix products, tile_block(): jnp.einsum('gjqck,ckgd->gjqcd', prob_bf, value_chosen, preferred_element_...  6.43 us
  transfers between devices with their start and end apart: 1, of which 1 were waited for; matrix products, arithmetic and copies ran while one was open for 0% of the time, Pallas kernels for 0%

commit v1 on v0

v1 whole, which is shorter than its diff:
```python
import functools
import math

import jax
import jax.numpy as jnp
from jax import lax
from jax.experimental import pallas as pl
from jax.experimental.pallas import tpu as pltpu
from jax.sharding import PartitionSpec as P

HD = 128
TILE = 128
NEGATIVE = -1e30
MESH = pl.DeviceIdType.MESH


def kernel(
    tok_count, head_count,
    mask_ref, q_hbm, k_hbm, v_hbm, w_hbm, out_hbm,
    kbuf, vbuf, q_buf, q_t, w_buf, row_max, row_sum, acc, attn,
    a_out, a_in, y_out, y_in, c_out, c_in, own_sum, result,
    local_sem, w_sem, out_sem, ring_send, ring_recv,
    a_send, a_recv, y_send, y_recv, c_send, c_recv,
):
    heads = q_t.shape[0]
    rows = q_buf.shape[0]
    tiles = rows // TILE
    pieces, _, piece = a_out.shape
    block = pieces * piece
    half = tok_count // 2
    scale = math.log2(math.e) / math.sqrt(HD)

    tok = lax.axis_index("tok")
    head = lax.axis_index("head")
    odd = lax.rem(tok, 2)
    place = (1 - odd) * (tok // 2) + odd * (tok_count - 1 - tok // 2)

    def tok_at(position):
        p = lax.rem(position + 2 * tok_count, tok_count)
        upper = p // half
        return (1 - upper) * (2 * p) + upper * (2 * (tok_count - 1 - p) + 1)

    right, left = tok_at(place + 1), tok_at(place - 1)
    mate = head + 1 - 2 * lax.rem(head, 2)
    across = lax.rem(head + head_count // 2, head_count)
    across_mate = lax.rem(mate + head_count // 2, head_count)

    k_copy = pltpu.make_async_copy(k_hbm, kbuf.at[tok], local_sem.at[0])
    v_copy = pltpu.make_async_copy(v_hbm, vbuf.at[tok], local_sem.at[1])
    q_copy = pltpu.make_async_copy(q_hbm, q_buf, local_sem.at[2])
    k_copy.start()
    v_copy.start()
    q_copy.start()
    w_copies = []
    for role, owner in enumerate((across_mate, across, mate, head)):
        columns = pl.ds(pl.multiple_of(owner * block, 128), block)
        w_copies.append(
            pltpu.make_async_copy(w_hbm.at[:, columns], w_buf.at[role], w_sem.at[role])
        )

    barrier = pltpu.get_barrier_semaphore()
    for peer in ((right, head), (left, head), (tok, mate), (tok, across)):
        pl.semaphore_signal(barrier, inc=1, device_id=peer, device_id_type=MESH)
    pl.semaphore_wait(barrier, 4)

    def message(direction, kind, step, owner):
        buf = (kbuf, vbuf)[kind]
        return pltpu.make_async_remote_copy(
            src_ref=buf.at[owner],
            dst_ref=buf.at[owner],
            send_sem=ring_send.at[direction, kind, step],
            recv_sem=ring_recv.at[direction, kind, step],
            device_id=((right, left)[direction], head),
            device_id_type=MESH,
        )

    k_copy.wait()
    message(0, 0, 0, tok).start()
    message(1, 0, 0, tok).start()
    v_copy.wait()
    message(0, 1, 0, tok).start()
    message(1, 1, 0, tok).start()
    for copy in w_copies:
        copy.start()
    q_copy.wait()
    for j in range(heads):
        q_t[j] = q_buf[:, j * HD:(j + 1) * HD].T
    row_max[...] = jnp.full_like(row_max, NEGATIVE)
    row_sum[...] = jnp.zeros_like(row_sum)
    acc[...] = jnp.zeros_like(acc)

    def absorb(owners):
        biases, turned = [], []
        for owner in owners:
            for t in range(tiles):
                parts = []
                for r in range(tiles):
                    kept = mask_ref[r, owner * tiles + t].astype(jnp.float32)
                    parts.append(jnp.full((1, TILE), (1.0 - kept) * NEGATIVE, jnp.float32))
                biases.append(jnp.concatenate(parts, axis=1))
            turned.append(vbuf[owner].T)
        for j in range(heads):
            scores = [
                jnp.dot(kbuf[owner], q_t[j], preferred_element_type=jnp.float32)
                for owner in owners
            ]
            pieces_of = [
                s[t * TILE:(t + 1) * TILE] for s in scores for t in range(tiles)
            ]
            old_max = row_max[j]
            new_max = old_max
            for s, bias in zip(pieces_of, biases):
                new_max = jnp.maximum(
                    new_max, jnp.max(s, axis=0, keepdims=True) * scale + bias
                )
            rescale = jnp.exp2(old_max - new_max)
            probs = [
                jnp.exp2(s * scale - (new_max - bias)) for s, bias in zip(pieces_of, biases)
            ]
            total = row_sum[j] * rescale
            for p in probs:
                total = total + jnp.sum(p, axis=0, keepdims=True)
            gathered = acc[j] * rescale
            for number in range(len(owners)):
                prob = jnp.concatenate(
                    [p.astype(jnp.bfloat16) for p in probs[number * tiles:(number + 1) * tiles]],
                    axis=0,
                )
                gathered = gathered + jnp.dot(
                    turned[number], prob, preferred_element_type=jnp.float32
                )
            row_max[j] = new_max
            row_sum[j] = total
            acc[j] = gathered

    absorb((tok,))

    def ring_step(step, carry):
        from_left, from_right = tok_at(place - 1 - step), tok_at(place + 1 + step)
        more = step + 1 < half - 1
        message(0, 0, step, from_left).wait_recv()
        message(0, 0, step + 1, from_left).start()
        message(1, 0, step, from_right).wait_recv()

        @pl.when(more)
        def _():
            message(1, 0, step + 1, from_right).start()

        message(0, 1, step, from_left).wait_recv()

        @pl.when(more)
        def _():
            message(0, 1, step + 1, from_left).start()

        message(1, 1, step, from_right).wait_recv()
        message(1, 1, step + 1, from_right).start()
        absorb((from_left, from_right))
        return carry

    lax.fori_loop(0, half - 1, ring_step, 0)
    far = tok_at(place + half)
    message(0, 0, half - 1, far).wait_recv()
    message(1, 1, half - 1, far).wait_recv()
    absorb((far,))

    for j in range(heads):
        attn[:, j * HD:(j + 1) * HD] = (acc[j] / row_sum[j]).T.astype(jnp.bfloat16)

    def product(role, i):
        columns = pl.ds(pl.multiple_of(i * piece, 128), piece)
        return jnp.dot(
            attn[...], w_buf[role, :, columns], preferred_element_type=jnp.float32
        )

    def hand(out, into, send, recv, i, peer):
        return pltpu.make_async_remote_copy(
            src_ref=out.at[i], dst_ref=into.at[i], send_sem=send.at[i], recv_sem=recv.at[i],
            device_id=(tok, peer), device_id_type=MESH,
        )

    hand_a = functools.partial(hand, a_out, a_in, a_send, a_recv)
    hand_y = functools.partial(hand, y_out, y_in, y_send, y_recv)
    hand_c = functools.partial(hand, c_out, c_in, c_send, c_recv)

    w_copies[0].wait()

    @pl.loop(0, pieces)
    def _(i):
        a_out[i] = product(0, i).astype(jnp.bfloat16)
        hand_a(i, mate).start()

    w_copies[1].wait()

    @pl.loop(0, pieces)
    def _(i):
        mine = product(1, i)
        hand_a(i, mate).wait_recv()
        y_out[i] = (mine + a_in[i].astype(jnp.float32)).astype(jnp.bfloat16)
        hand_y(i, across).start()

    w_copies[2].wait()

    @pl.loop(0, pieces)
    def _(i):
        c_out[i] = product(2, i).astype(jnp.bfloat16)
        hand_c(i, mate).start()

    w_copies[3].wait()

    @pl.loop(0, pieces)
    def _(i):
        mine = product(3, i)
        hand_c(i, mate).wait_recv()
        own_sum[i] = mine + c_in[i].astype(jnp.float32)

    def store(i):
        columns = pl.ds(pl.multiple_of(i * piece, 128), piece)
        return pltpu.make_async_copy(result.at[i], out_hbm.at[:, columns], out_sem.at[i])

    @pl.loop(0, pieces)
    def _(i):
        hand_y(i, across).wait_recv()
        result[i] = (own_sum[i] + y_in[i].astype(jnp.float32)).astype(jnp.bfloat16)
        store(i).start()

    @pl.loop(0, half - 1)
    def _(step):
        for direction in range(2):
            for kind in range(2):
                message(direction, kind, step, tok).wait_send()

    message(0, 0, half - 1, tok).wait_send()
    message(1, 1, half - 1, tok).wait_send()

    @pl.loop(0, pieces)
    def _(i):
        hand_a(i, mate).wait_send()
        hand_c(i, mate).wait_send()
        hand_y(i, across).wait_send()
        store(i).wait()


def per_device(tok_count, head_count, queries, key_rows, value_rows, tile_mask, out_weight):
    rows, width = queries.shape
    heads = width // HD
    block = out_weight.shape[1] // head_count
    piece = math.gcd(block, 2 * TILE)
    pieces = block // piece
    half = tok_count // 2
    bf16, f32 = jnp.bfloat16, jnp.float32
    dma = pltpu.SemaphoreType.DMA
    part = pltpu.VMEM((pieces, rows, piece), bf16)
    anywhere = pl.BlockSpec(memory_space=pl.ANY)
    return pl.pallas_call(
        functools.partial(kernel, tok_count, head_count),
        out_shape=jax.ShapeDtypeStruct((rows, block), bf16),
        in_specs=[pl.BlockSpec(memory_space=pltpu.SMEM)] + [anywhere] * 4,
        out_specs=anywhere,
        scratch_shapes=[
            pltpu.VMEM((tok_count, rows, HD), bf16),
            pltpu.VMEM((tok_count, rows, HD), bf16),
            pltpu.VMEM((rows, width), bf16),
            pltpu.VMEM((heads, HD, rows), bf16),
            pltpu.VMEM((head_count, width, block), bf16),
            pltpu.VMEM((heads, 1, rows), f32),
            pltpu.VMEM((heads, 1, rows), f32),
            pltpu.VMEM((heads, HD, rows), f32),
            pltpu.VMEM((rows, width), bf16),
            part, part, part, part, part, part,
            pltpu.VMEM((pieces, rows, piece), f32),
            part,
            dma((3,)), dma((head_count,)), dma((pieces,)),
            dma((2, 2, half)), dma((2, 2, half)),
            dma((pieces,)), dma((pieces,)), dma((pieces,)),
            dma((pieces,)), dma((pieces,)), dma((pieces,)),
        ],
        compiler_params=pltpu.CompilerParams(collective_id=0, has_side_effects=True),
    )(tile_mask, queries, key_rows, value_rows, out_weight)


def solution(mesh):
    tok_count, head_count = mesh.shape["tok"], mesh.shape["head"]
    assert head_count == 4 and tok_count % 2 == 0
    return jax.shard_map(
        functools.partial(per_device, tok_count, head_count),
        mesh=mesh,
        in_specs=(
            P("tok", "head"),
            P("tok", "head"),
            P("tok", "head"),
            P("tok", None),
            P("head", None),
        ),
        out_specs=P("tok", "head"),
        check_vma=False,
    )
```

time: 161 us -> 47.4 us (0.29)
  blocking collectives: 64.7 us -> 0 us
  Pallas kernels: 0 us -> 45.2 us
  waiting for transfers between devices: 39.2 us -> 0 us
  matrix products: 21.4 us -> 0 us
  other arithmetic: 16 us -> 0 us
  between operations: 14.9 us -> 0.01 us
  local copies, waits for them, and re-layouts: 4.9 us -> 2.06 us
    all_gather x2 -> x0, blocking collectives: 64.7 us -> none  [the longest x1 33.3 us: per_device(): lax.all_gather(value_rows, 'tok', axis=0, tiled=True)]
    pallas_call x0 -> x1, Pallas kernels: none -> 45.2 us  [per_device(): pl.pallas_call(functools.partial(kernel, tok_count, head_count), out_shap...]
    reduce_scatter x1 -> x0, waiting for transfers between devices: 39.2 us -> none  [per_device(): lax.psum_scatter(lax.dot_general(out_weight, attention, (((0,), (1,)), ((...]
    dot_general x5 -> x0, matrix products: 21.4 us -> none  [the longest x1 7.67 us: per_device(): lax.dot_general(out_weight, attention, (((0,), (1,)), ((), ())), preferre...]
    reduce_sum x4 -> x0, other arithmetic: 9.32 us -> none  [the longest x2 9.13 us: tile_block(): tile_sums = jnp.sum(prob_bf.astype(jnp.float32), axis=-1)]
    sort x2 -> x0, other arithmetic: 2.62 us -> none  [sweep_piece(): ordering = jnp.argsort(1 - living, stable=True)]
    gather x4 -> x0, local copies, waits for them, and re-layouts: 2.59 us -> none  [the longest x2 1.3 us: one_turn(): jnp.take(key_tiles, picked, axis=0)]
    unnamed x2 -> x1, local copies, waits for them, and re-layouts: 0.32 us -> 2.06 us
  transfers between devices with their start and end apart: 1 -> 0, of which waited for: 1 -> 0; matrix products, arithmetic and copies ran while one was open for 0% -> 0% of each run, Pallas kernels for 0% -> 0%
where the time goes in v1:
time: 47.4 us; the launch traced here: 47.3 us
  Pallas kernels  45.2 us (95%)
  local copies, waits for them, and re-layouts  2.06 us (4%)
    pallas_call x1, Pallas kernels, per_device(): pl.pallas_call(functools.partial(kernel, tok_count, head_count), out_shap...  45.2 us
    unnamed x1, local copies, waits for them, and re-layouts  2.06 us

profile of v1, /device:TPU:0, one launch (start us, length us, event | category | flops | bytes accessed | tf_op | source)
XLA Modules:
  0.0 47.3 jit_solution(589361095577224861)
XLA Ops:
  0.0 45.2 %shard_map.55 = bf16[256,1536]{1,0:T(8,128)(2,1)} custom-call(s32[2,16]{1,0:T(2,128)} %mask_ref.1, bf16[256,768]{1,0:T(8,128)(2,1)} %q_hbm.1, bf16[256,128]{1,0:T(8,128)(2,1)} %k_hbm.1, bf16[256,128]{1,0:T(8,128)(2,1)} %v_hbm.1, bf16[768,6144]{1,0:T(8,128)(2,1)} %w_hbm.1), custom_call_target="tpu_custom_call" | custom-call | tf_op jit(solution)/shard_map/pallas_call | solution.py:254
  45.2 2.1 %copy.7 = bf16[256,1536]{1,0:T(8,128)(2,1)} copy(bf16[256,1536]{1,0:T(8,128)(2,1)} %shard_map.55) | data formatting | bytes 1572864

commit v2 on v1

--- a/solution.py
+++ b/solution.py
@@ -63,23 +63,26 @@
         pl.semaphore_signal(barrier, inc=1, device_id=peer, device_id_type=MESH)
     pl.semaphore_wait(barrier, 4)
 
-    def message(direction, kind, step, owner):
-        buf = (kbuf, vbuf)[kind]
+    def message(direction, part, step, owner):
+        buf = (kbuf, vbuf)[part // 2]
+        lines = pl.ds(part % 2 * (rows // 2), rows // 2)
         return pltpu.make_async_remote_copy(
-            src_ref=buf.at[owner],
-            dst_ref=buf.at[owner],
-            send_sem=ring_send.at[direction, kind, step],
-            recv_sem=ring_recv.at[direction, kind, step],
+            src_ref=buf.at[owner, lines],
+            dst_ref=buf.at[owner, lines],
+            send_sem=ring_send.at[direction, part, step],
+            recv_sem=ring_recv.at[direction, part, step],
             device_id=((right, left)[direction], head),
             device_id_type=MESH,
         )
 
     k_copy.wait()
-    message(0, 0, 0, tok).start()
-    message(1, 0, 0, tok).start()
+    for part in range(2):
+        message(0, part, 0, tok).start()
+        message(1, part, 0, tok).start()
     v_copy.wait()
-    message(0, 1, 0, tok).start()
-    message(1, 1, 0, tok).start()
+    for part in range(2, 4):
+        message(0, part, 0, tok).start()
+        message(1, part, 0, tok).start()
     for copy in w_copies:
         copy.start()
     q_copy.wait()
@@ -90,7 +93,8 @@
     acc[...] = jnp.zeros_like(acc)
 
     def absorb(owners):
-        biases, turned = [], []
+        turned = [vbuf[owner].T for owner in owners]
+        biases = []
         for owner in owners:
             for t in range(tiles):
                 parts = []
@@ -98,7 +102,6 @@
                     kept = mask_ref[r, owner * tiles + t].astype(jnp.float32)
                     parts.append(jnp.full((1, TILE), (1.0 - kept) * NEGATIVE, jnp.float32))
                 biases.append(jnp.concatenate(parts, axis=1))
-            turned.append(vbuf[owner].T)
         for j in range(heads):
             scores = [
                 jnp.dot(kbuf[owner], q_t[j], preferred_element_type=jnp.float32)
@@ -135,32 +138,24 @@
 
     absorb((tok,))
 
-    def ring_step(step, carry):
-        from_left, from_right = tok_at(place - 1 - step), tok_at(place + 1 + step)
+    @pl.loop(0, half - 1)
+    def _(step):
+        arriving = tok_at(place - 1 - step), tok_at(place + 1 + step)
         more = step + 1 < half - 1
-        message(0, 0, step, from_left).wait_recv()
-        message(0, 0, step + 1, from_left).start()
-        message(1, 0, step, from_right).wait_recv()
-
-        @pl.when(more)
-        def _():
-            message(1, 0, step + 1, from_right).start()
-
-        message(0, 1, step, from_left).wait_recv()
-
-        @pl.when(more)
-        def _():
-            message(0, 1, step + 1, from_left).start()
-
-        message(1, 1, step, from_right).wait_recv()
-        message(1, 1, step + 1, from_right).start()
-        absorb((from_left, from_right))
-        return carry
-
-    lax.fori_loop(0, half - 1, ring_step, 0)
+        for part in range(4):
+            for direction in range(2):
+                message(direction, part, step, arriving[direction]).wait_recv()
+                onward = message(direction, part, step + 1, arriving[direction])
+                if part // 2 == direction:
+                    onward.start()
+                else:
+                    pl.when(more)(onward.start)
+        absorb(arriving)
+
     far = tok_at(place + half)
-    message(0, 0, half - 1, far).wait_recv()
-    message(1, 1, half - 1, far).wait_recv()
+    for part in range(2):
+        message(0, part, half - 1, far).wait_recv()
+        message(1, part + 2, half - 1, far).wait_recv()
     absorb((far,))
 
     for j in range(heads):
@@ -182,22 +177,28 @@
     hand_y = functools.partial(hand, y_out, y_in, y_send, y_recv)
     hand_c = functools.partial(hand, c_out, c_in, c_send, c_recv)
 
-    w_copies[0].wait()
-
-    @pl.loop(0, pieces)
-    def _(i):
+    def give(i):
         a_out[i] = product(0, i).astype(jnp.bfloat16)
         hand_a(i, mate).start()
 
-    w_copies[1].wait()
-
-    @pl.loop(0, pieces)
-    def _(i):
+    def cross(i):
         mine = product(1, i)
         hand_a(i, mate).wait_recv()
         y_out[i] = (mine + a_in[i].astype(jnp.float32)).astype(jnp.bfloat16)
         hand_y(i, across).start()
 
+    ahead = min(4, pieces)
+    w_copies[0].wait()
+    pl.loop(0, ahead)(give)
+    w_copies[1].wait()
+
+    @pl.loop(ahead, pieces)
+    def _(i):
+        cross(i - ahead)
+        give(i)
+
+    pl.loop(pieces - ahead, pieces)(cross)
+
     w_copies[2].wait()
 
     @pl.loop(0, pieces)
@@ -226,11 +227,12 @@
     @pl.loop(0, half - 1)
     def _(step):
         for direction in range(2):
-            for kind in range(2):
-                message(direction, kind, step, tok).wait_send()
-
-    message(0, 0, half - 1, tok).wait_send()
-    message(1, 1, half - 1, tok).wait_send()
+            for part in range(4):
+                message(direction, part, step, tok).wait_send()
+
+    for part in range(2):
+        message(0, part, half - 1, tok).wait_send()
+        message(1, part + 2, half - 1, tok).wait_send()
 
     @pl.loop(0, pieces)
     def _(i):
@@ -270,7 +272,7 @@
             pltpu.VMEM((pieces, rows, piece), f32),
             part,
             dma((3,)), dma((head_count,)), dma((pieces,)),
-            dma((2, 2, half)), dma((2, 2, half)),
+            dma((2, 4, half)), dma((2, 4, half)),
             dma((pieces,)), dma((pieces,)), dma((pieces,)),
             dma((pieces,)), dma((pieces,)), dma((pieces,)),
         ],
@@ -280,7 +282,7 @@
 
 def solution(mesh):
     tok_count, head_count = mesh.shape["tok"], mesh.shape["head"]
-    assert head_count == 4 and tok_count % 2 == 0
+    assert head_count == 4 and tok_count % 2 == 0 and tok_count >= 4
     return jax.shard_map(
         functools.partial(per_device, tok_count, head_count),
         mesh=mesh,

time: 47.4 us -> 46.5 us (0.981)
  Pallas kernels: 45.2 us -> 44.3 us
    pallas_call x1, Pallas kernels: 45.2 us -> 44.3 us  [per_device(): pl.pallas_call(functools.partial(kernel, tok_count, head_count), out_shap...]
where the time goes in v2:
time: 46.5 us; the launch traced here: 46.3 us
  Pallas kernels  44.3 us (95%)
  local copies, waits for them, and re-layouts  2.06 us (4%)
    pallas_call x1, Pallas kernels, per_device(): pl.pallas_call(functools.partial(kernel, tok_count, head_count), out_shap...  44.3 us
    unnamed x1, local copies, waits for them, and re-layouts  2.06 us

profile of v2, /device:TPU:0, one launch (start us, length us, event | category | flops | bytes accessed | tf_op | source)
XLA Modules:
  0.0 46.3 jit_solution(7160840923311486810)
XLA Ops:
  0.0 44.3 %shard_map.55 = bf16[256,1536]{1,0:T(8,128)(2,1)} custom-call(s32[2,16]{1,0:T(2,128)} %mask_ref.1, bf16[256,768]{1,0:T(8,128)(2,1)} %q_hbm.1, bf16[256,128]{1,0:T(8,128)(2,1)} %k_hbm.1, bf16[256,128]{1,0:T(8,128)(2,1)} %v_hbm.1, bf16[768,6144]{1,0:T(8,128)(2,1)} %w_hbm.1), custom_call_target="tpu_custom_call" | custom-call | tf_op jit(solution)/shard_map/pallas_call | solution.py:256
  44.3 2.1 %copy.7 = bf16[256,1536]{1,0:T(8,128)(2,1)} copy(bf16[256,1536]{1,0:T(8,128)(2,1)} %shard_map.55) | data formatting | bytes 1572864
